TPU v7x, 32 devices: a whole 2x2x4 slice. The times are simulated.
32 devices in a mesh: expert: 8 (over y, x, core), dp: 4 (over z).
Axes of the slice: x: 2, y: 2, z: 4, core: 2. Of those that a mesh axis runs over, the one named last changes fastest.
Arguments:
- tokens: bfloat16 [4096, 2048], P(('expert', 'dp')), may hold values from -6 to 6
- expert_ids: int32 [4096, 4], P(('expert', 'dp')), may hold values from 0 to 15, all different within a row; in each aligned block of 128 rows (0 to 127, 128 to 255, ...) at most 96 rows name the same one
- gate_probs: float32 [4096, 4], P(('expert', 'dp')), may hold values from 0.05 to 0.5
- expert_weights: bfloat16 [2048, 3, 16, 384], P(None, None, 'expert'), may hold values from -0.125 to 0.125
- out_grad: bfloat16 [4096, 2048], P(('expert', 'dp')), may hold values from -1.5 to 1.5
Outputs:
- layer_out: bfloat16 [4096, 2048], P(('expert', 'dp'))
- token_grad: bfloat16 [4096, 2048], P(('expert', 'dp'))
- gate_grad: float32 [4096, 4], P(('expert', 'dp'))
- weight_grad: float32 [2048, 3, 16, 384], P('dp', None, 'expert')
Inputs may be any that keep to these rules, and one draw needn't show every extreme that they name: `expert_ids`: each row names 4 different experts. Among the 128 rows of one device (aligned blocks of rows), no expert is named by more than 96 rows, and in some block some expert is named by exactly 96 rows.
All inputs are finite; a program needn't handle non-finite values.
Results may differ from a plain program's by a relative error of at most 0.0085.
Values may be sent and summed in bfloat16 or wider, within the bound.
A program may use at most 128 MiB of HBM per device.

v0:
```python
import jax
import jax.numpy as jnp
from jax import lax
from jax.sharding import PartitionSpec as P

F32 = jnp.float32
BF16 = jnp.bfloat16


def dot(a, b, ca, cb):
    return lax.dot_general(a, b, (((ca,), (cb,)), ((), ())), preferred_element_type=F32)


def local(tokens, expert_ids, gate_probs, expert_weights, out_grad):
    tok_count, top_count = expert_ids.shape
    d = tokens.shape[1]
    ranks = lax.axis_size("expert")
    me = lax.axis_index("expert")
    local_experts, h = expert_weights.shape[2:]
    n = ranks * tok_count
    eh = local_experts * h
    x = lax.all_gather(tokens, "expert", axis=0, tiled=True)
    small = jnp.concatenate([expert_ids.astype(F32), gate_probs], axis=1)
    small = lax.all_gather(small, "expert", axis=0, tiled=True)
    g = lax.all_gather(out_grad, "expert", axis=0, tiled=True)
    ids = small[:, :top_count].astype(jnp.int32)
    probs = small[:, top_count:]
    mine = me * local_experts + jnp.arange(local_experts, dtype=jnp.int32)
    hit = ids[:, :, None] == mine[None, None, :]
    p = jnp.sum(jnp.where(hit, probs[:, :, None], 0.0), axis=1)
    w = expert_weights.reshape(d, 3 * eh)
    wgu = w[:, : 2 * eh]
    wd = w[:, 2 * eh :]
    a = dot(x, wgu, 1, 0)
    gate = a[:, :eh].reshape(n, local_experts, h)
    up = a[:, eh:].reshape(n, local_experts, h)
    s = jax.nn.sigmoid(gate)
    hidden = gate * s * up
    ph = (p[:, :, None] * hidden).astype(BF16).reshape(n, eh)
    lpart = dot(ph, wd, 1, 1).astype(BF16)
    layer_out = lax.psum_scatter(lpart, "expert", scatter_dimension=0, tiled=True)
    wd_grad = dot(g, ph, 0, 0).astype(BF16)
    wd_grad = lax.psum_scatter(wd_grad, "dp", scatter_dimension=0, tiled=True)
    u = dot(g, wd, 1, 0).reshape(n, local_experts, h)
    gg = jnp.sum(u * hidden, axis=-1)
    hc = p[:, :, None] * u
    gc = (hc * up * s * (1.0 + gate * (1.0 - s))).astype(BF16).reshape(n, eh)
    uc = (hc * gate * s).astype(BF16).reshape(n, eh)
    cots = jnp.concatenate([gc, uc], axis=1)
    tpart = dot(cots, wgu, 1, 1).astype(BF16)
    token_grad = lax.psum_scatter(tpart, "expert", scatter_dimension=0, tiled=True)
    ggk = jnp.sum(jnp.where(hit, gg[:, None, :], 0.0), axis=2)
    gate_grad = lax.psum_scatter(ggk, "expert", scatter_dimension=0, tiled=True)
    wgu_grad = dot(x, cots, 0, 0).astype(BF16)
    wgu_grad = lax.psum_scatter(wgu_grad, "dp", scatter_dimension=0, tiled=True)
    wg = jnp.concatenate([wgu_grad, wd_grad], axis=1)
    weight_grad = wg.astype(F32).reshape(-1, 3, local_experts, h)
    return (layer_out, token_grad, gate_grad, weight_grad)


def solution(mesh):
    tok = P(("expert", "dp"), None)
    wsp = P(None, None, "expert", None)
    return jax.shard_map(
        local,
        mesh=mesh,
        in_specs=(tok, tok, tok, wsp, tok),
        out_specs=(tok, tok, tok, P("dp", None, "expert", None)),
        check_vma=False,
    )
```

profile of v0, /device:TPU:0, one launch (start us, length us, event | category | flops | bytes accessed | tf_op | source)
XLA Modules:
  0.0 438.3 jit_solution(9271335342334902050)
XLA Ops:
  8.7 20.9 %reshape.38 = bf16[2048,2304]{1,0:T(8,128)(2,1)} reshape(bf16[2048,3,2,384]{3,2,1,0:T(2,128)(2,1)} %param.8) | data formatting | bytes 18874368 | tf_op jit(solution)/shard_map/reshape | solution.py:31
  29.6 10.5 %all_gather.9 = f32[1024,8]{0,1:T(8,128)S(1)} all-gather(f32[128,8]{0,1:T(8,128)S(1)} %pad_maximum_fusion.4), channel_id=1, replica_groups=mesh['expert'=8,'dp'=4] {'expert'}, dimensions={0}, use_global_device_ids=true | all-gather | bytes 36864 | tf_op jit(solution)/shard_map/all_gather | solution.py:24
  40.1 9.2 %all-gather.3.cloned.1.call-done = bf16[1024,2048]{1,0:T(8,128)(2,1)} async-done(((bf16[128,2048]{1,0:T(8,128)(2,1)}), bf16[1024,2048]{1,0:T(8,128)(2,1)}) %all-gather.3.cloned.1.call-update) | async-done | bytes 4194320 | tf_op jit(solution)/shard_map/all_gather | solution.py:22
  49.4 10.0 %fusion.3 = f32[1024,1536]{1,0:T(8,128)S(1)} fusion(bf16[1024,2048]{1,0:T(8,128)(2,1)} %all-gather.3.cloned.1.call-done, bf16[2048,2304]{1,0:T(8,128)(2,1)} %reshape.38), kind=kOutput, calls=%fused_computation.4 | convolution fusion | flops 6442450944 | bytes 16777216 | tf_op jit(solution)/shard_map/dot_general | solution.py:11
  59.4 3.5 fusion.16
  64.5 2.4 copy.35
  66.9 2.5 copy.37
  69.3 2.4 copy.38
  71.7 2.4 copy.39
  74.1 13.9 %all-gather.5.cloned.1.call-done = bf16[1024,2048]{1,0:T(8,128)(2,1)} async-done(((bf16[128,2048]{1,0:T(8,128)(2,1)}), bf16[1024,2048]{1,0:T(8,128)(2,1)}) %all-gather.5.cloned.1.call-update) | async-done | bytes 4194320 | tf_op jit(solution)/shard_map/all_gather | solution.py:25
  88.0 6.3 %fusion.9 = f32[1024,768]{0,1:T(8,128)S(1)} fusion(bf16[1024,2048]{1,0:T(8,128)(2,1)} %all-gather.5.cloned.1.call-done, bf16[2048,2304]{1,0:T(8,128)(2,1)} %reshape.38), kind=kOutput, calls=%fused_computation.16 | convolution fusion | flops 3221225472 | bytes 10485760 | tf_op jit(solution)/shard_map/dot_general | solution.py:11
  94.3 2.4 copy.34
  99.1 4.8 %multiply_reduce_fusion = f32[1024,2]{0,1:T(2,128)S(1)} fusion(f32[1024,2,384]{2,0,1:T(8,128)} %copy.40, f32[1024,2,384]{2,0,1:T(8,128)} %copy.39, f32[1024,2,384]{2,0,1:T(8,128)} %copy.37), kind=kLoop, calls=%fused_computation.10 | loop fusion | flops 5502976 | bytes 9445376 | tf_op jit(solution)/shard_map/reduce_sum | solution.py:45
  104.2 2.4 mul.62
  109.9 6.0 %multiply_convert_fusion.1 = (bf16[1024,768]{1,0:T(8,128)(2,1)}, bf16[1024,768]{1,0:T(8,128)(2,1)}, bf16[1024,768]{1,0:T(8,128)(2,1)S(1)}) fusion(f32[1024,768]{1,0:T(8,128)} %bitcast.22, f32[1024,768]{1,0:T(8,128)S(1)} %copy-done.1, f32[1024,1536]{1,0:T(8,128)} %copy-done), kind=kLoop, calls=%fused_computation.12 | loop fusion | flops 14155776 | bytes 17301504 | tf_op jit(solution)/shard_map/convert_element_type | solution.py:47
  117.1 4.8 %fusion.8 = bf16[2048,768]{0,1:T(8,128)(2,1)} fusion(bf16[1024,768]{1,0:T(8,128)(2,1)S(1)} %get-tuple-element.32, bf16[1024,2048]{1,0:T(8,128)(2,1)S(1)} %copy-done.8), kind=kOutput, calls=%fused_computation.15 | convolution fusion | flops 3222798336 | bytes 8912896 | tf_op jit(solution)/shard_map/dot_general | solution.py:11
  123.8 10.9 %fusion = bf16[2048,1536]{0,1:T(8,128)(2,1)} fusion(bf16[1024,2048]{1,0:T(8,128)(2,1)} %all-gather.3.cloned.1.call-done, bf16[1024,768]{1,0:T(8,128)(2,1)S(1)} %copy-done.5, bf16[1024,768]{1,0:T(8,128)(2,1)S(1)} %copy-done.4), kind=kOutput, calls=%fused_computation.1 | convolution fusion | flops 6451888128 | bytes 13631488 | tf_op jit(solution)/shard_map/dot_general | solution.py:11
  134.8 11.0 %fusion.5 = bf16[1024,2048]{1,0:T(8,128)(2,1)} fusion(bf16[2048,2304]{1,0:T(8,128)(2,1)} %reshape.38, bf16[1024,768]{1,0:T(8,128)(2,1)S(1)} %copy-done.5, bf16[1024,768]{1,0:T(8,128)(2,1)S(1)} %copy-done.4), kind=kOutput, calls=%fused_computation.6 | convolution fusion | flops 6450839552 | bytes 13631488 | tf_op jit(solution)/shard_map/dot_general | solution.py:11
  147.2 6.9 %convolution_convert_fusion.1 = bf16[1024,2048]{1,0:T(8,128)(2,1)} fusion(bf16[1024,768]{1,0:T(8,128)(2,1)S(1)} %copy-done.3, bf16[2048,2304]{1,0:T(8,128)(2,1)} %reshape.38), kind=kOutput, calls=%fused_computation.7 | convolution fusion | flops 3223322624 | bytes 8912896 | tf_op jit(solution)/shard_map/dot_general | solution.py:11
  155.6 51.5 %reduce-scatter.14.cloned.1.call-done = bf16[512,768]{0,1:T(8,128)(2,1)} async-done(((bf16[2048,768]{0,1:T(8,128)(2,1)}), bf16[512,768]{0,1:T(8,128)(2,1)}) %reduce-scatter.14.cloned.1.call-update) | async-done | bytes 786448 | tf_op jit(solution)/shard_map/reduce_scatter | solution.py:43
  207.1 113.1 %reduce-scatter.12.cloned.1.call-done = bf16[512,1536]{0,1:T(8,128)(2,1)} async-done(((bf16[2048,1536]{0,1:T(8,128)(2,1)}), bf16[512,1536]{0,1:T(8,128)(2,1)}) %reduce-scatter.12.cloned.1.call-update) | async-done | bytes 1572880 | tf_op jit(solution)/shard_map/reduce_scatter | solution.py:55
  321.9 4.8 %copy.43 = f32[512,3,2,384]{3,2,1,0:T(2,128)} copy(bf16[512,3,2,384]{0,3,2,1:T(8,128)(2,1)S(1)} %bitcast.23) | data formatting | bytes 7077888
  326.7 49.5 %reduce-scatter.10.cloned.1.call-done = bf16[128,2048]{1,0:T(8,128)(2,1)} async-done(((bf16[1024,2048]{1,0:T(8,128)(2,1)}), bf16[128,2048]{1,0:T(8,128)(2,1)}) %reduce-scatter.10.cloned.1.call-update) | async-done | bytes 524304 | tf_op jit(solution)/shard_map/reduce_scatter | solution.py:51
  376.2 55.3 %reduce-scatter.8.cloned.1.call-done = bf16[128,2048]{1,0:T(8,128)(2,1)} async-done(((bf16[1024,2048]{1,0:T(8,128)(2,1)}), bf16[128,2048]{1,0:T(8,128)(2,1)}) %reduce-scatter.8.cloned.1.call-update) | async-done | bytes 524304 | tf_op jit(solution)/shard_map/reduce_scatter | solution.py:41
  (44 shorter events, 16.8 us)
Async XLA Ops:
  7.2 42.2 %all-gather.3.cloned.1.call-start = ((), (), s32[]{:S(2)}) async-start(), calls=%async_computation.5 | async-start | bytes 4718592 | tf_op jit(solution)/shard_map/all_gather | solution.py:22
  7.9 80.1 %all-gather.5.cloned.1.call-start = ((), (), s32[]{:S(2)}) async-start(), calls=%async_computation.7 | async-start | bytes 4718592 | tf_op jit(solution)/shard_map/all_gather | solution.py:25
  8.6 145.5 %reduce-scatter.16.cloned.1.call-start = ((), (), s32[]{:S(2)}) async-start(), calls=%async_computation.11 | async-start | bytes 589824
  8.7 20.9 %copy-start.6 = (s32[128,4]{0,1:T(4,128)S(1)}, s32[128,4]{0,1:T(4,128)}, u32[]{:S(2)}) copy-start(s32[128,4]{0,1:T(4,128)} %param.6) | copy-start | bytes 6148
  8.7 20.9 %copy-start.7 = (f32[128,4]{0,1:T(4,128)S(1)}, f32[128,4]{0,1:T(4,128)}, u32[]{:S(2)}) copy-start(f32[128,4]{0,1:T(4,128)} %param.7) | copy-start | bytes 6148
  59.4 5.1 %copy-start = (f32[1024,1536]{1,0:T(8,128)}, f32[1024,1536]{1,0:T(8,128)S(1)}, u32[]{:S(2)}) copy-start(f32[1024,1536]{1,0:T(8,128)S(1)} %fusion.3) | copy-start | bytes 18874372
  106.7 3.2 copy-start.1
  109.6 97.4 %reduce-scatter.14.cloned.1.call-start = ((), (), s32[]{:S(2)}) async-start(), calls=%async_computation.10 | async-start | bytes 3932160 | tf_op jit(solution)/shard_map/reduce_scatter | solution.py:43
  109.9 7.2 %copy-start.8 = (bf16[1024,2048]{1,0:T(8,128)(2,1)S(1)}, bf16[1024,2048]{1,0:T(8,128)(2,1)}, u32[]{:S(2)}) copy-start(bf16[1024,2048]{1,0:T(8,128)(2,1)} %all-gather.5.cloned.1.call-done) | copy-start | bytes 12582916
  115.9 1.1 copy-start.2
  121.9 1.4 copy-start.4
  121.9 1.9 copy-start.5
  121.9 198.2 %reduce-scatter.12.cloned.1.call-start = ((), (), s32[]{:S(2)}) async-start(), calls=%async_computation.9 | async-start | bytes 7864320 | tf_op jit(solution)/shard_map/reduce_scatter | solution.py:55
  134.7 241.5 %reduce-scatter.10.cloned.1.call-start = ((), (), s32[]{:S(2)}) async-start(), calls=%async_computation.8 | async-start | bytes 4718592 | tf_op jit(solution)/shard_map/reduce_scatter | solution.py:51
  145.8 1.4 copy-start.3
  145.8 285.7 %reduce-scatter.8.cloned.1.call-start = ((), (), s32[]{:S(2)}) async-start(), calls=%async_computation.6 | async-start | bytes 4718592 | tf_op jit(solution)/shard_map/reduce_scatter | solution.py:41
Sparse Core Ops, SparseCore 0:
  9.9 39.4 all-gather.2
  51.3 36.6 all-gather.4
  109.8 34.1 reduce-scatter.15
  146.8 60.2 reduce-scatter.13
  209.3 110.7 reduce-scatter.11
  324.3 51.8 reduce-scatter.9
  380.1 51.3 reduce-scatter.7
where the time goes:
time: 439 us; the launch traced here: 438 us
  waiting for transfers between devices  294 us (67%)
  local copies, waits for them, and re-layouts  56.4 us (13%)
  matrix products  49.9 us (11%)
  between operations  14.3 us (3%)
  other arithmetic  12.8 us (3%)
  blocking collectives  10.5 us (2%)
    reduce_scatter x1, waiting for transfers between devices, local(): wgu_grad = lax.psum_scatter(wgu_grad, 'dp', scatter_dimension=0, tiled=True)  113 us
    reduce_scatter x1, waiting for transfers between devices, local(): lax.psum_scatter(lpart, 'expert', scatter_dimension=0, tiled=True)  55.3 us
    reduce_scatter x1, waiting for transfers between devices, local(): wd_grad = lax.psum_scatter(wd_grad, 'dp', scatter_dimension=0, tiled=True)  51.5 us
    dot_general x6, matrix products, dot(): lax.dot_general(a, b, (((ca,), (cb,)), ((), ())), preferred_element_type=...  49.9 us
    reduce_scatter x1, waiting for transfers between devices, local(): lax.psum_scatter(tpart, 'expert', scatter_dimension=0, tiled=True)  49.5 us
    reshape x1, local copies, waits for them, and re-layouts, local(): w = expert_weights.reshape(d, 3 * eh)  20.9 us
    unnamed x22, local copies, waits for them, and re-layouts  15.1 us
    all_gather x1, waiting for transfers between devices, local(): g = lax.all_gather(out_grad, 'expert', axis=0, tiled=True)  13.9 us
  transfers between devices with their start and end apart: 7, of which 6 were waited for; matrix products, arithmetic and copies ran while one was open for 21% of the time, Pallas kernels for 0%

commit v1 on v0

--- a/solution.py
+++ b/solution.py
@@ -21,7 +21,14 @@
     eh = local_experts * h
     x = lax.all_gather(tokens, "expert", axis=0, tiled=True)
     small = jnp.concatenate([expert_ids.astype(F32), gate_probs], axis=1)
-    small = lax.all_gather(small, "expert", axis=0, tiled=True)
+    ring = [small]
+    for hop in range(7):
+        ring.append(lax.ppermute(ring[-1], "expert", [(dev, (dev + 1) % 8) for dev in range(8)]))
+    small = jnp.roll(
+        jnp.concatenate(ring[::-1], axis=0),
+        (lax.axis_index("expert") + 1) * ring[0].shape[0],
+        axis=0,
+    )
     g = lax.all_gather(out_grad, "expert", axis=0, tiled=True)
     ids = small[:, :top_count].astype(jnp.int32)
     probs = small[:, top_count:]

time: 439 us -> 439 us (level)
  blocking collectives: 10.5 us -> 0 us
  waiting for transfers between devices: 294 us -> 302 us
    ppermute x0 -> x7, waiting for transfers between devices: none -> 23.9 us  [local(): lax.ppermute(ring[-1], 'expert', [(dev, (dev + 1) % 8) for dev in range(8)])]
    all_gather x1 -> x0, blocking collectives: 10.5 us -> none  [local(): small = lax.all_gather(small, 'expert', axis=0, tiled=True)]
    all_gather x1, waiting for transfers between devices: 9.23 us -> 0.01 us  [local(): x = lax.all_gather(tokens, 'expert', axis=0, tiled=True)]
    all_gather x1, waiting for transfers between devices: 13.9 us -> 7.36 us  [local(): g = lax.all_gather(out_grad, 'expert', axis=0, tiled=True)]
    unnamed x22 -> x34, local copies, waits for them, and re-layouts: 15.1 us -> 15.2 us
  transfers between devices with their start and end apart: 7 -> 14, of which waited for: 6 -> 11; matrix products, arithmetic and copies ran while one was open for 21% -> 21% of each run, Pallas kernels for 0% -> 0%
where the time goes in v1:
time: 439 us; the launch traced here: 438 us
  waiting for transfers between devices  302 us (69%)
  local copies, waits for them, and re-layouts  56.5 us (13%)
  matrix products  50.1 us (11%)
  between operations  14.4 us (3%)
  other arithmetic  14.2 us (3%)
    reduce_scatter x1, waiting for transfers between devices, local(): wgu_grad = lax.psum_scatter(wgu_grad, 'dp', scatter_dimension=0, tiled=True)  113 us
    reduce_scatter x1, waiting for transfers between devices, local(): lax.psum_scatter(lpart, 'expert', scatter_dimension=0, tiled=True)  55.3 us
    reduce_scatter x1, waiting for transfers between devices, local(): wd_grad = lax.psum_scatter(wd_grad, 'dp', scatter_dimension=0, tiled=True)  51.4 us
    dot_general x6, matrix products, dot(): lax.dot_general(a, b, (((ca,), (cb,)), ((), ())), preferred_element_type=...  50.1 us
    reduce_scatter x1, waiting for transfers between devices, local(): lax.psum_scatter(tpart, 'expert', scatter_dimension=0, tiled=True)  49.5 us
    ppermute x7, waiting for transfers between devices, local(): lax.ppermute(ring[-1], 'expert', [(dev, (dev + 1) % 8) for dev in range(8)])  23.9 us
    reshape x1, local copies, waits for them, and re-layouts, local(): w = expert_weights.reshape(d, 3 * eh)  20.8 us
    unnamed x34, local copies, waits for them, and re-layouts  15.2 us
  transfers between devices with their start and end apart: 14, of which 11 were waited for; matrix products, arithmetic and copies ran while one was open for 21% of the time, Pallas kernels for 0%

profile of v1, /device:TPU:0, one launch (start us, length us, event | category | flops | bytes accessed | tf_op | source)
XLA Modules:
  0.0 438.2 jit_solution(2509097387834566184)
XLA Ops:
  10.5 4.2 collective-permute-done
  14.7 3.9 collective-permute-done.1
  18.6 3.9 collective-permute-done.2
  22.6 4.0 collective-permute-done.3
  26.6 3.9 collective-permute-done.4
  30.5 3.9 collective-permute-done.5
  34.5 20.8 %reshape.38 = bf16[2048,2304]{1,0:T(8,128)(2,1)} reshape(bf16[2048,3,2,384]{3,2,1,0:T(2,128)(2,1)} %param.8) | data formatting | bytes 18874368 | tf_op jit(solution)/shard_map/reshape | solution.py:38
  55.6 10.3 %fusion.3 = f32[1024,1536]{1,0:T(8,128)S(1)} fusion(bf16[1024,2048]{1,0:T(8,128)(2,1)} %all-gather.3.cloned.1.call-done, bf16[2048,2304]{1,0:T(8,128)(2,1)} %reshape.38), kind=kOutput, calls=%fused_computation.4 | convolution fusion | flops 6442450944 | bytes 16777216 | tf_op jit(solution)/shard_map/dot_general | solution.py:11
  65.8 3.5 fusion.16
  73.4 2.5 copy.37
  80.6 7.4 %all-gather.5.cloned.1.call-done = bf16[1024,2048]{1,0:T(8,128)(2,1)} async-done(((bf16[128,2048]{1,0:T(8,128)(2,1)}), bf16[1024,2048]{1,0:T(8,128)(2,1)}) %all-gather.5.cloned.1.call-update) | async-done | bytes 4194320 | tf_op jit(solution)/shard_map/all_gather | solution.py:32
  88.0 6.2 %fusion.9 = f32[1024,768]{0,1:T(8,128)S(1)} fusion(bf16[1024,2048]{1,0:T(8,128)(2,1)} %all-gather.5.cloned.1.call-done, bf16[2048,2304]{1,0:T(8,128)(2,1)} %reshape.38), kind=kOutput, calls=%fused_computation.16 | convolution fusion | flops 3221225472 | bytes 10485760 | tf_op jit(solution)/shard_map/dot_general | solution.py:11
  99.0 4.8 %multiply_reduce_fusion = f32[1024,2]{0,1:T(2,128)S(1)} fusion(f32[1024,2,384]{2,0,1:T(8,128)} %copy.40, f32[1024,2,384]{2,0,1:T(8,128)} %copy.39, f32[1024,2,384]{2,0,1:T(8,128)} %copy.37), kind=kLoop, calls=%fused_computation.10 | loop fusion | flops 5502976 | bytes 9445376 | tf_op jit(solution)/shard_map/reduce_sum | solution.py:52
  104.1 2.4 mul.66
  109.8 6.0 %multiply_convert_fusion.1 = (bf16[1024,768]{1,0:T(8,128)(2,1)}, bf16[1024,768]{1,0:T(8,128)(2,1)}, bf16[1024,768]{1,0:T(8,128)(2,1)S(1)}) fusion(f32[1024,768]{1,0:T(8,128)} %bitcast.22, f32[1024,768]{1,0:T(8,128)S(1)} %copy-done.1, f32[1024,1536]{1,0:T(8,128)} %copy-done), kind=kLoop, calls=%fused_computation.12 | loop fusion | flops 14155776 | bytes 17301504 | tf_op jit(solution)/shard_map/convert_element_type | solution.py:54
  117.0 4.8 %fusion.8 = bf16[2048,768]{0,1:T(8,128)(2,1)} fusion(bf16[1024,768]{1,0:T(8,128)(2,1)S(1)} %get-tuple-element.32, bf16[1024,2048]{1,0:T(8,128)(2,1)S(1)} %copy-done.7), kind=kOutput, calls=%fused_computation.15 | convolution fusion | flops 3222798336 | bytes 8912896 | tf_op jit(solution)/shard_map/dot_general | solution.py:11
  123.7 10.9 %fusion = bf16[2048,1536]{0,1:T(8,128)(2,1)} fusion(bf16[1024,2048]{1,0:T(8,128)(2,1)} %all-gather.3.cloned.1.call-done, bf16[1024,768]{1,0:T(8,128)(2,1)S(1)} %copy-done.5, bf16[1024,768]{1,0:T(8,128)(2,1)S(1)} %copy-done.4), kind=kOutput, calls=%fused_computation.1 | convolution fusion | flops 6451888128 | bytes 13631488 | tf_op jit(solution)/shard_map/dot_general | solution.py:11
  134.7 11.0 %fusion.5 = bf16[1024,2048]{1,0:T(8,128)(2,1)} fusion(bf16[2048,2304]{1,0:T(8,128)(2,1)} %reshape.38, bf16[1024,768]{1,0:T(8,128)(2,1)S(1)} %copy-done.5, bf16[1024,768]{1,0:T(8,128)(2,1)S(1)} %copy-done.4), kind=kOutput, calls=%fused_computation.6 | convolution fusion | flops 6450839552 | bytes 13631488 | tf_op jit(solution)/shard_map/dot_general | solution.py:11
  147.1 6.9 %convolution_convert_fusion.1 = bf16[1024,2048]{1,0:T(8,128)(2,1)} fusion(bf16[1024,768]{1,0:T(8,128)(2,1)S(1)} %copy-done.3, bf16[2048,2304]{1,0:T(8,128)(2,1)} %reshape.38), kind=kOutput, calls=%fused_computation.7 | convolution fusion | flops 3223322624 | bytes 8912896 | tf_op jit(solution)/shard_map/dot_general | solution.py:11
  155.5 51.4 %reduce-scatter.14.cloned.1.call-done = bf16[512,768]{0,1:T(8,128)(2,1)} async-done(((bf16[2048,768]{0,1:T(8,128)(2,1)}), bf16[512,768]{0,1:T(8,128)(2,1)}) %reduce-scatter.14.cloned.1.call-update) | async-done | bytes 786448 | tf_op jit(solution)/shard_map/reduce_scatter | solution.py:50
  207.0 113.1 %reduce-scatter.12.cloned.1.call-done = bf16[512,1536]{0,1:T(8,128)(2,1)} async-done(((bf16[2048,1536]{0,1:T(8,128)(2,1)}), bf16[512,1536]{0,1:T(8,128)(2,1)}) %reduce-scatter.12.cloned.1.call-update) | async-done | bytes 1572880 | tf_op jit(solution)/shard_map/reduce_scatter | solution.py:62
  321.8 4.8 %copy.43 = f32[512,3,2,384]{3,2,1,0:T(2,128)} copy(bf16[512,3,2,384]{0,3,2,1:T(8,128)(2,1)S(1)} %bitcast.23) | data formatting | bytes 7077888
  326.6 49.5 %reduce-scatter.10.cloned.1.call-done = bf16[128,2048]{1,0:T(8,128)(2,1)} async-done(((bf16[1024,2048]{1,0:T(8,128)(2,1)}), bf16[128,2048]{1,0:T(8,128)(2,1)}) %reduce-scatter.10.cloned.1.call-update) | async-done | bytes 524304 | tf_op jit(solution)/shard_map/reduce_scatter | solution.py:58
  376.1 55.3 %reduce-scatter.8.cloned.1.call-done = bf16[128,2048]{1,0:T(8,128)(2,1)} async-done(((bf16[1024,2048]{1,0:T(8,128)(2,1)}), bf16[128,2048]{1,0:T(8,128)(2,1)}) %reduce-scatter.8.cloned.1.call-update) | async-done | bytes 524304 | tf_op jit(solution)/shard_map/reduce_scatter | solution.py:48
  (71 shorter events, 28.4 us)
Async XLA Ops:
  7.2 48.4 %all-gather.3.cloned.1.call-start = ((), (), s32[]{:S(2)}) async-start(), calls=%async_computation.5 | async-start | bytes 4718592 | tf_op jit(solution)/shard_map/all_gather | solution.py:22
  7.9 80.1 %all-gather.5.cloned.1.call-start = ((), (), s32[]{:S(2)}) async-start(), calls=%async_computation.7 | async-start | bytes 4718592 | tf_op jit(solution)/shard_map/all_gather | solution.py:32
  8.6 145.4 %reduce-scatter.16.cloned.1.call-start = ((), (), s32[]{:S(2)}) async-start(), calls=%async_computation.11 | async-start | bytes 589824
  10.1 4.6 %collective-permute-start = (f32[128,8]{0,1:T(8,128)S(1)}, f32[128,8]{0,1:T(8,128)S(1)}, u32[]{:S(2)}, u32[]{:S(2)}) collective-permute-start(f32[128,8]{0,1:T(8,128)S(1)} %pad_maximum_fusion.4), channel_id=1, source_target_pairs={{0,4},{4,8},{8,12},{12,16},{16,20},{20,24},{24,28},{28,0},{1,5},{5... | collective-permute-start | bytes 12296 | tf_op jit(solution)/shard_map/ppermute | solution.py:26
  14.7 3.9 collective-permute-start.1
  18.6 3.9 collective-permute-start.2
  22.6 4.0 collective-permute-start.3
  26.6 3.9 collective-permute-start.4
  30.5 3.9 collective-permute-start.5
  34.5 20.8 %collective-permute-start.6 = (f32[128,8]{0,1:T(8,128)S(1)}, f32[128,8]{0,1:T(8,128)S(1)}, u32[]{:S(2)}, u32[]{:S(2)}) collective-permute-start(f32[128,8]{0,1:T(8,128)S(1)} %collective-permute-done.5), channel_id=1, source_target_pairs={{0,4},{4,8},{8,12},{12,16},{16,20},{20,24},{24,28},{28,0},{1,5},{5... | collective-permute-start | bytes 12296 | tf_op jit(solution)/shard_map/ppermute | solution.py:26
  34.5 20.9 %copy-start.6 = (f32[128,4]{0,1:T(4,128)S(1)}, f32[128,4]{0,1:T(4,128)}, u32[]{:S(2)}) copy-start(f32[128,4]{0,1:T(4,128)} %param.7) | copy-start | bytes 6148
  65.8 5.2 %copy-start = (f32[1024,1536]{1,0:T(8,128)}, f32[1024,1536]{1,0:T(8,128)S(1)}, u32[]{:S(2)}) copy-start(f32[1024,1536]{1,0:T(8,128)S(1)} %fusion.3) | copy-start | bytes 18874372
  106.6 3.2 copy-start.1
  109.5 97.4 %reduce-scatter.14.cloned.1.call-start = ((), (), s32[]{:S(2)}) async-start(), calls=%async_computation.10 | async-start | bytes 3932160 | tf_op jit(solution)/shard_map/reduce_scatter | solution.py:50
  109.8 7.2 %copy-start.7 = (bf16[1024,2048]{1,0:T(8,128)(2,1)S(1)}, bf16[1024,2048]{1,0:T(8,128)(2,1)}, u32[]{:S(2)}) copy-start(bf16[1024,2048]{1,0:T(8,128)(2,1)} %all-gather.5.cloned.1.call-done) | copy-start | bytes 12582916
  115.8 1.2 copy-start.2
  121.8 1.4 copy-start.4
  121.8 1.9 copy-start.5
  121.8 198.2 %reduce-scatter.12.cloned.1.call-start = ((), (), s32[]{:S(2)}) async-start(), calls=%async_computation.9 | async-start | bytes 7864320 | tf_op jit(solution)/shard_map/reduce_scatter | solution.py:62
  134.6 241.5 %reduce-scatter.10.cloned.1.call-start = ((), (), s32[]{:S(2)}) async-start(), calls=%async_computation.8 | async-start | bytes 4718592 | tf_op jit(solution)/shard_map/reduce_scatter | solution.py:58
  145.7 1.4 copy-start.3
  145.7 285.6 %reduce-scatter.8.cloned.1.call-start = ((), (), s32[]{:S(2)}) async-start(), calls=%async_computation.6 | async-start | bytes 4718592 | tf_op jit(solution)/shard_map/reduce_scatter | solution.py:48
Sparse Core Ops, SparseCore 0:
  9.9 39.4 all-gather.2
  51.3 36.6 all-gather.4
  109.7 34.1 reduce-scatter.15
  146.7 60.2 reduce-scatter.13
  209.2 110.7 reduce-scatter.11
  324.2 51.8 reduce-scatter.9
  380.0 51.2 reduce-scatter.7
